TPU v7x, 256 devices: a whole 4x4x8 slice. The times are simulated.
256 devices in a mesh: dp: 8 (over x, core), graph: 32 (over z, y).
Axes of the slice: x: 4, y: 4, z: 8, core: 2. Of those that a mesh axis runs over, the one named last changes fastest.
Arguments:
- feats: bfloat16 [8, 16384, 512], P('dp', 'graph'), may hold values from -6 to 6
- grad_out: bfloat16 [8, 16384, 512], P('dp', 'graph'), may hold values from -6 to 6
- w_self: bfloat16 [512, 512], replicated, may hold values from -0.25 to 0.25
- w_neigh: bfloat16 [512, 512], replicated, may hold values from -0.25 to 0.25
- nbr: int32 [8, 16384, 10], P('dp', 'graph'), may hold values from 0 to 2047, as said below
- deg: int32 [8, 16384], P('dp', 'graph'), may hold values from 1 to 10
- hub_rows: int32 [8, 512], P('dp', 'graph'), may hold values from 0 to 511, as said below
- send_rows: int32 [8, 32, 32, 32], P('dp', 'graph'), may hold values from 0 to 511
Outputs:
- out: bfloat16 [8, 16384, 512], P('dp', 'graph')
- grad_feats: bfloat16 [8, 16384, 512], P('dp', 'graph')
- grad_w_self: float32 [512, 512], P('graph')
- grad_w_neigh: float32 [512, 512], P('graph')
Inputs may be any that keep to these rules, and one draw needn't show every extreme that they name: `hub_rows`: within each partition's block of 16 entries the rows are distinct rows of that partition. `nbr`: entries name rows of the partition's table: below 512 its own rows, then 512 hub rows, then 1024 received rows. Only slots below deg are live.
All inputs are finite; a program needn't handle non-finite values.
Results may differ from a plain program's by a relative error of at most 0.007.
Values may be sent and summed in bfloat16 or wider, within the bound.
A program may use at most 64 MiB of HBM per device.

v0:
```python
import jax
import jax.numpy as jnp
from jax import lax
from jax.sharding import PartitionSpec as P


def shards(feats, grad_out, w_self, w_neigh, nbr, deg, hub_rows, send_rows):
    own = feats[0]
    grads = grad_out[0]
    rows, width = own.shape
    idx = nbr[0]
    dcount = deg[0]
    hub_idx = hub_rows[0]
    sent_idx = send_rows[0, 0]
    hub_local = own[hub_idx]
    hubs = lax.all_gather(hub_local, "graph", axis=0, tiled=True)
    outgoing = own[sent_idx]
    incoming = lax.all_to_all(outgoing, "graph", split_axis=0, concat_axis=0, tiled=True)
    nhub = hubs.shape[0]
    table = jnp.concatenate([own, hubs, incoming.reshape(-1, width)], axis=0)
    slots = idx.shape[1]
    live = jnp.arange(slots)[None, :] < dcount[:, None]
    total = jnp.zeros((rows, width), jnp.float32)
    for k in range(slots):
        total = total + jnp.where(live[:, k : k + 1], table[idx[:, k]].astype(jnp.float32), 0.0)
    degree = dcount.astype(jnp.float32)[:, None]
    agg = (total / degree).astype(jnp.bfloat16)
    result = (
        jnp.dot(own, w_self, preferred_element_type=jnp.float32)
        + jnp.dot(agg, w_neigh, preferred_element_type=jnp.float32)
    ).astype(jnp.bfloat16)
    trans = (((1,), (1,)), ((), ()))
    back = lax.dot_general(grads, w_neigh, trans, preferred_element_type=jnp.float32) / degree
    height = table.shape[0]
    dtable = jnp.zeros((height, width), jnp.float32)
    for k in range(slots):
        target = jnp.where(live[:, k], idx[:, k], height)
        dtable = dtable.at[target].add(back, mode="drop")
    hub_back = lax.psum_scatter(
        dtable[rows : rows + nhub].astype(jnp.bfloat16), "graph", scatter_dimension=0, tiled=True
    ).astype(jnp.float32)
    recv_back = lax.all_to_all(
        dtable[rows + nhub :].reshape(incoming.shape).astype(jnp.bfloat16),
        "graph",
        split_axis=0,
        concat_axis=0,
        tiled=True,
    ).astype(jnp.float32)
    inner = (((0,), (0,)), ((), ()))
    dws = lax.dot_general(own, grads, inner, preferred_element_type=jnp.float32)
    dwn = lax.dot_general(agg, grads, inner, preferred_element_type=jnp.float32)
    dlocal = (
        lax.dot_general(grads, w_self, trans, preferred_element_type=jnp.float32) + dtable[:rows]
    )
    dlocal = dlocal.at[hub_idx].add(hub_back)
    dlocal = dlocal.at[sent_idx.reshape(-1)].add(recv_back.reshape(-1, width))
    grad_rows = dlocal.astype(jnp.bfloat16)
    share = width // lax.axis_size("graph")
    sum_self, sum_neigh = lax.psum((dws, dwn), ("dp", "graph"))
    start = lax.axis_index("graph") * share
    sum_self = lax.dynamic_slice_in_dim(sum_self, start, share, 0)
    sum_neigh = lax.dynamic_slice_in_dim(sum_neigh, start, share, 0)
    count = lax.axis_size("dp") * lax.axis_size("graph") * rows
    scale = 1.0 / jnp.sqrt(jnp.float32(count))
    return (result[None], grad_rows[None], sum_self * scale, sum_neigh * scale)


def solution(mesh):
    placed = (
        P("dp", "graph", None),
        P("dp", "graph", None),
        P(),
        P(),
        P("dp", "graph", None),
        P("dp", "graph"),
        P("dp", "graph"),
        P("dp", "graph", None, None),
    )
    return jax.shard_map(
        shards,
        mesh=mesh,
        in_specs=placed,
        out_specs=(
            P("dp", "graph", None),
            P("dp", "graph", None),
            P("graph", None),
            P("graph", None),
        ),
        check_vma=False,
    )
```

profile of v0, /device:TPU:1, one launch (start us, length us, event | category | flops | bytes accessed | tf_op | source)
XLA Modules:
  0.0 480.9 jit_solution(7234979474906921619)
XLA Ops:
  8.9 6.3 %gather_fusion.1 = bf16[1024,512]{1,0:T(8,128)(2,1)} fusion(bf16[512,512]{1,0:T(8,128)(2,1)} %bitcast.64, s32[1024]{0:T(1024)S(1)} %broadcast_clamp_fusion), kind=kCustom, calls=%fused_computation.1 | custom fusion | bytes 2101248 | tf_op jit(solution)/shard_map/gather | solution.py:17
  15.2 12.2 %all-to-all-start = ((bf16[32,32,512]{2,1,0:T(8,128)(2,1)}), bf16[32,32,512]{2,1,0:T(8,128)(2,1)}, u32[]{:S(2)}, u32[]{:S(2)}) async-start(bf16[32,32,512]{2,1,0:T(8,128)(2,1)} %bitcast.5), calls=%async_computation | async-start | bytes 2097152 | tf_op jit(solution)/shard_map/all_to_all | solution.py:18
  28.0 5.7 %scatter_custom_fusion = f32[2048,512]{1,0:T(8,128)} fusion(s32[512]{0:T(512)S(1)} %bitcast.92, f32[512,512]{1,0:T(8,128)S(1)} %convolution_divide_fusion, f32[]{:T(128)} %constant.10.clone.1), kind=kCustom, calls=%fused_computation.27 | custom fusion | flops 262144 | bytes 4194308 | tf_op jit(solution)/shard_map/scatter-add | solution.py:38
  33.7 7.6 %scatter_fusion = f32[2048,512]{1,0:T(8,128)} fusion(f32[2048,512]{1,0:T(8,128)} %scatter_custom_fusion, s32[512]{0:T(512)S(1)} %bitcast.77, f32[512,512]{1,0:T(8,128)S(1)} %convolution_divide_fusion), kind=kCustom, calls=%fused_computation.13 | custom fusion | flops 262144 | bytes 3147776 | tf_op jit(solution)/shard_map/scatter-add | solution.py:38
  41.4 7.8 %scatter_fusion.1 = f32[2048,512]{1,0:T(8,128)} fusion(f32[2048,512]{1,0:T(8,128)} %scatter_fusion, s32[512]{0:T(512)S(1)} %bitcast.76, f32[512,512]{1,0:T(8,128)S(1)} %convolution_divide_fusion), kind=kCustom, calls=%fused_computation.14 | custom fusion | flops 262144 | bytes 3147776 | tf_op jit(solution)/shard_map/scatter-add | solution.py:38
  49.2 7.6 %scatter_fusion.2 = f32[2048,512]{1,0:T(8,128)} fusion(f32[2048,512]{1,0:T(8,128)} %scatter_fusion.1, s32[512]{0:T(512)S(1)} %bitcast.75, f32[512,512]{1,0:T(8,128)S(1)} %convolution_divide_fusion), kind=kCustom, calls=%fused_computation.15 | custom fusion | flops 262144 | bytes 3147776 | tf_op jit(solution)/shard_map/scatter-add | solution.py:38
  56.8 7.6 %scatter_fusion.3 = f32[2048,512]{1,0:T(8,128)} fusion(f32[2048,512]{1,0:T(8,128)} %scatter_fusion.2, s32[512]{0:T(512)S(1)} %bitcast.74, f32[512,512]{1,0:T(8,128)S(1)} %convolution_divide_fusion), kind=kCustom, calls=%fused_computation.16 | custom fusion | flops 262144 | bytes 3147776 | tf_op jit(solution)/shard_map/scatter-add | solution.py:38
  64.4 7.6 %scatter_fusion.4 = f32[2048,512]{1,0:T(8,128)} fusion(f32[2048,512]{1,0:T(8,128)} %scatter_fusion.3, s32[512]{0:T(512)S(1)} %bitcast.73, f32[512,512]{1,0:T(8,128)S(1)} %convolution_divide_fusion), kind=kCustom, calls=%fused_computation.17 | custom fusion | flops 262144 | bytes 3147776 | tf_op jit(solution)/shard_map/scatter-add | solution.py:38
  72.1 7.8 %scatter_fusion.5 = f32[2048,512]{1,0:T(8,128)} fusion(f32[2048,512]{1,0:T(8,128)} %scatter_fusion.4, s32[512]{0:T(512)S(1)} %bitcast.72, f32[512,512]{1,0:T(8,128)S(1)} %convolution_divide_fusion), kind=kCustom, calls=%fused_computation.18 | custom fusion | flops 262144 | bytes 3147776 | tf_op jit(solution)/shard_map/scatter-add | solution.py:38
  79.9 7.6 %scatter_fusion.6 = f32[2048,512]{1,0:T(8,128)} fusion(f32[2048,512]{1,0:T(8,128)} %scatter_fusion.5, s32[512]{0:T(512)S(1)} %bitcast.71, f32[512,512]{1,0:T(8,128)S(1)} %convolution_divide_fusion), kind=kCustom, calls=%fused_computation.19 | custom fusion | flops 262144 | bytes 3147776 | tf_op jit(solution)/shard_map/scatter-add | solution.py:38
  87.6 7.6 %scatter_fusion.7 = f32[2048,512]{1,0:T(8,128)} fusion(f32[2048,512]{1,0:T(8,128)} %scatter_fusion.6, s32[512]{0:T(512)S(1)} %bitcast.78, f32[512,512]{1,0:T(8,128)S(1)} %convolution_divide_fusion), kind=kCustom, calls=%fused_computation.20 | custom fusion | flops 262144 | bytes 3147776 | tf_op jit(solution)/shard_map/scatter-add | solution.py:38
  95.2 7.6 %scatter_fusion.8 = f32[2048,512]{1,0:T(8,128)} fusion(f32[2048,512]{1,0:T(8,128)} %scatter_fusion.7, s32[512]{0:T(512)S(1)} %bitcast.70, f32[512,512]{1,0:T(8,128)S(1)} %convolution_divide_fusion), kind=kCustom, calls=%fused_computation.21 | custom fusion | flops 262144 | bytes 3147776 | tf_op jit(solution)/shard_map/scatter-add | solution.py:38
  102.9 2.5 convert.5
  108.2 43.9 %all-gather = bf16[512,512]{1,0:T(8,128)(2,1)} all-gather(bf16[16,512]{1,0:T(8,128)(2,1)S(1)} %gather_fusion), channel_id=2, replica_groups=mesh['dp'=8,'graph'=32] {'graph'}, dimensions={0}, use_global_device_ids=true | all-gather | bytes 540672 | tf_op jit(solution)/shard_map/all_gather | solution.py:16
  152.2 5.9 %all-to-all-start.1 = ((bf16[32,32,512]{2,1,0:T(8,128)(2,1)}), bf16[32,32,512]{2,1,0:T(8,128)(2,1)}, u32[]{:S(2)}, u32[]{:S(2)}) async-start(bf16[32,32,512]{2,1,0:T(8,128)(2,1)} %bitcast.67), calls=%async_computation.2 | async-start | bytes 2097152 | tf_op jit(solution)/shard_map/all_to_all | solution.py:42
  159.9 1.5 pad_maximum_fusion
  161.4 2.6 gather_fusion.10
  164.0 2.6 gather_fusion.11
  166.6 2.6 gather_fusion.2
  169.2 2.6 gather_fusion.3
  171.9 2.6 gather_fusion.4
  174.5 2.6 gather_fusion.5
  177.1 2.6 gather_fusion.6
  179.8 2.6 gather_fusion.7
  182.4 2.6 gather_fusion.8
  185.0 2.6 gather_fusion.9
  187.6 4.1 divide_convert_fusion
  194.6 1.8 convolution_add_fusion
  196.4 124.8 %reduce-scatter.2.cloned.1.call-done = bf16[16,512]{1,0:T(8,128)(2,1)} async-done(((bf16[512,512]{1,0:T(8,128)(2,1)}), bf16[16,512]{1,0:T(8,128)(2,1)}) %reduce-scatter.2.cloned.1.call-update) | async-done | bytes 16400 | tf_op jit(solution)/shard_map/reduce_scatter | solution.py:39
  322.5 7.9 %scatter_custom_fusion.11 = f32[512,512]{1,0:T(8,128)S(1)} fusion(f32[512,512]{1,0:T(8,128)S(1)} %scatter_custom_fusion.10, s32[1024]{0:T(1024)S(1)} %bitcast.91, bf16[1024,512]{1,0:T(8,128)(2,1)} %bitcast.33), kind=kCustom, calls=%fused_computation.25 | custom fusion | flops 1048576 | bytes 2097152 | tf_op jit(solution)/shard_map/scatter-add | solution.py:56
  330.4 2.5 fusion.5
  333.7 137.9 %all-reduce.3.cloned.1.call-done = (f32[512,512]{1,0:T(8,128)}, f32[512,512]{1,0:T(8,128)}) async-done(((f32[512,512]{1,0:T(8,128)}, f32[512,512]{1,0:T(8,128)}), (f32[512,512]{1,0:T(8,128)}, f32[512,512]{1,0:T(8,128)})) %all-reduce.3.cloned.1.call-update) | async-done | bytes 2097168 | tf_op jit(solution)/shard_map/psum | solution.py:59
  (57 shorter events, 12.4 us)
Async XLA Ops:
  8.0 19.5 %copy-start = (bf16[1,512,512]{2,1,0:T(8,128)(2,1)S(1)}, bf16[1,512,512]{2,1,0:T(8,128)(2,1)}, u32[]{:S(2)}) copy-start(bf16[1,512,512]{2,1,0:T(8,128)(2,1)} %param.9) | copy-start | bytes 1572868
  8.9 18.5 %copy-start.7 = (s32[1,512]{1,0:T(1,128)S(1)}, s32[1,512]{1,0:T(1,128)}, u32[]{:S(2)}) copy-start(s32[1,512]{1,0:T(1,128)} %param.13) | copy-start | bytes 6148
  8.9 18.5 %copy-start.6 = (s32[1,512,10]{1,0,2:T(1,128)S(1)}, s32[1,512,10]{1,0,2:T(1,128)}, u32[]{:S(2)}) copy-start(s32[1,512,10]{1,0,2:T(1,128)} %param.12) | copy-start | bytes 61444
  8.9 18.6 %copy-start.3 = (bf16[512,512]{1,0:T(8,128)(2,1)S(1)}, bf16[512,512]{1,0:T(8,128)(2,1)}, u32[]{:S(2)}) copy-start(bf16[512,512]{1,0:T(8,128)(2,1)} %param.11) | copy-start | bytes 1572868
  15.2 137.0 %all-to-all-start = ((bf16[32,32,512]{2,1,0:T(8,128)(2,1)}), bf16[32,32,512]{2,1,0:T(8,128)(2,1)}, u32[]{:S(2)}, u32[]{:S(2)}) async-start(bf16[32,32,512]{2,1,0:T(8,128)(2,1)} %bitcast.5), calls=%async_computation | async-start | bytes 2097152 | tf_op jit(solution)/shard_map/all_to_all | solution.py:18
  27.3 293.8 %reduce-scatter.2.cloned.1.call-start = ((), (), s32[]{:S(2)}) async-start(), calls=%async_computation.3 | async-start | bytes 540672 | tf_op jit(solution)/shard_map/reduce_scatter | solution.py:39
  102.9 4.4 copy-start.5
  102.9 4.5 copy-start.8
  102.9 4.5 copy-start.1
  152.2 170.3 %all-to-all-start.1 = ((bf16[32,32,512]{2,1,0:T(8,128)(2,1)}), bf16[32,32,512]{2,1,0:T(8,128)(2,1)}, u32[]{:S(2)}, u32[]{:S(2)}) async-start(bf16[32,32,512]{2,1,0:T(8,128)(2,1)} %bitcast.67), calls=%async_computation.2 | async-start | bytes 2097152 | tf_op jit(solution)/shard_map/all_to_all | solution.py:42
  158.1 313.5 %all-reduce.3.cloned.1.call-start = ((), (), s32[]{:S(2)}) async-start(), calls=%async_computation.4 | async-start | bytes 4194304 | tf_op jit(solution)/shard_map/psum | solution.py:59
  187.6 5.6 %copy-start.2 = (bf16[512,512]{1,0:T(8,128)(2,1)S(1)}, bf16[512,512]{1,0:T(8,128)(2,1)}, u32[]{:S(2)}) copy-start(bf16[512,512]{1,0:T(8,128)(2,1)} %param.10) | copy-start | bytes 1572868
  194.6 135.7 %copy-start.4 = (bf16[512,512]{1,0:T(8,128)(2,1)S(1)}, bf16[512,512]{1,0:T(8,128)(2,1)}, u32[]{:S(2)}) copy-start(bf16[512,512]{1,0:T(8,128)(2,1)} %param.11) | copy-start | bytes 1572868
Sparse Core Ops, SparseCore 0:
  106.4 214.7 reduce-scatter.1
Sparse Core Ops, SparseCore 1:
  193.3 278.2 all-reduce.2
where the time goes:
time: 490 us; the launch traced here: 481 us
  waiting for transfers between devices  263 us (54%)
  other arithmetic  95.4 us (19%)
  blocking collectives  43.9 us (9%)
  local copies, waits for them, and re-layouts  35.2 us (7%)
  starting transfers between devices  18.4 us (4%)
  between operations  16.3 us (3%)
  matrix products  9.02 us (2%)
    psum x1, waiting for transfers between devices, shards(): sum_self, sum_neigh = lax.psum((dws, dwn), ('dp', 'graph'))  138 us
    reduce_scatter x1, waiting for transfers between devices, shards(): lax.psum_scatter(dtable[rows:rows + nhub].astype(jnp.bfloat16), 'graph',...  125 us
    scatter-add x10, other arithmetic, shards(): dtable = dtable.at[target].add(back, mode='drop')  74.8 us
    all_gather x1, blocking collectives, shards(): hubs = lax.all_gather(hub_local, 'graph', axis=0, tiled=True)  43.9 us
    gather x10, local copies, waits for them, and re-layouts, shards(): table[idx[:, k]].astype(jnp.float32)  26.2 us
    all_to_all x1, starting transfers between devices, shards(): lax.all_to_all(outgoing, 'graph', split_axis=0, concat_axis=0, tiled=True)  12.2 us
  transfers between devices with their start and end apart: 4, of which 2 were waited for; matrix products, arithmetic and copies ran while one was open for 27% of the time, Pallas kernels for 0%

commit v1 on v0

v1 whole, which is shorter than its diff:
```python
import functools

import jax
import jax.numpy as jnp
from jax import lax
from jax.experimental import pallas as pl
from jax.experimental.pallas import tpu as pltpu
from jax.sharding import PartitionSpec as P

F32 = jnp.float32
BF16 = jnp.bfloat16
TRANS = (((1,), (1,)), ((), ()))
INNER = (((0,), (0,)), ((), ()))


def dot(a, b, dims=(((1,), (0,)), ((), ()))):
    return lax.dot_general(a, b, dims, preferred_element_type=F32)


def layer_kernel(
    parts,
    groups,
    scale,
    own_ref,
    g_ref,
    ws_ref,
    wn_ref,
    nbr_ref,
    deg_ref,
    idx_ref,
    out_ref,
    gf_ref,
    gws_ref,
    gwn_ref,
    live_ref,
    pick_ref,
    spread_ref,
    count_t_ref,
    count_ref,
    send_ref,
    hub_ref,
    recv_ref,
    hubs_ref,
    hi_ref,
    lo_ref,
    dlocal_ref,
    back_send_ref,
    back_hub_ref,
    back_recv_ref,
    back_hubs_ref,
    base_ref,
    agg_ref,
    inv_ref,
    dw_ref,
    dw_recv_ref,
    slab_ref,
    slab_recv_ref,
    fin_ref,
    fin_recv_ref,
    f_send,
    f_recv,
    fh_send,
    fh_recv,
    b_send,
    b_recv,
    bh_send,
    bh_recv,
    w_send,
    w_recv,
    s_send,
    s_recv,
    e_send,
    e_recv,
):
    rows, width = own_ref.shape
    slots = nbr_ref.shape[0]
    cap = recv_ref.shape[0] // parts
    hub = hubs_ref.shape[0] // parts
    sent = recv_ref.shape[0]
    lanes = 128
    me = lax.axis_index("graph")
    lane = lax.axis_index("dp")
    height = count_t_ref.shape[0]

    def graph_peer(k):
        return lax.rem(me + k, parts)

    def dp_peer(k):
        return lax.rem(lane + k, groups)

    barrier = pltpu.get_barrier_semaphore()

    @pl.loop(1, parts)
    def _(k):
        pl.semaphore_signal(barrier, inc=1, device_id={"graph": graph_peer(k)})

    @pl.loop(1, groups)
    def _(k):
        pl.semaphore_signal(barrier, inc=1, device_id={"dp": dp_peer(k)})

    def column(row, n=lanes):
        return jnp.transpose(jnp.broadcast_to(row, (n, lanes)))

    lane_iota = lax.broadcasted_iota(jnp.int32, (lanes, lanes), 1)
    for i in range(sent // lanes + 1):
        spot = column(idx_ref[i : i + 1, :])
        tall = lanes if i < sent // lanes else hub
        for j in range(width // lanes):
            hit = (spot == lane_iota + lanes * j).astype(F32).astype(BF16)
            pick_ref[lanes * i : lanes * i + tall, lanes * j : lanes * (j + 1)] = hit[:tall]
    for i in range(sent // 256):
        send_ref[256 * i : 256 * (i + 1), :] = dot(
            pick_ref[256 * i : 256 * (i + 1), :], own_ref[...]
        ).astype(BF16)
    hub_ref[...] = dot(pick_ref[sent : sent + hub, :], own_ref[...]).astype(BF16)

    pl.semaphore_wait(barrier, parts - 1 + groups - 1)

    def exchange(k, src, dst, ssem, rsem, size, shared):
        q = graph_peer(k)
        return pltpu.make_async_remote_copy(
            src_ref=src if shared else src.at[pl.ds(pl.multiple_of(q * size, size), size)],
            dst_ref=dst.at[pl.ds(pl.multiple_of(me * size, size), size)],
            send_sem=ssem.at[k],
            recv_sem=rsem.at[k],
            device_id={"graph": q},
        )

    def arrival(k, dst, ssem, rsem, size):
        q = lax.rem(me + parts - k, parts)
        spot = dst.at[pl.ds(pl.multiple_of(q * size, size), size)]
        return pltpu.make_async_remote_copy(
            src_ref=spot,
            dst_ref=spot,
            send_sem=ssem.at[k],
            recv_sem=rsem.at[k],
            device_id={"graph": graph_peer(k)},
        )

    @pl.loop(1, parts)
    def _(k):
        exchange(k, send_ref, recv_ref, f_send, f_recv, cap, False).start()
        exchange(k, hub_ref, hubs_ref, fh_send, fh_recv, hub, True).start()

    recv_ref[pl.ds(pl.multiple_of(me * cap, cap), cap), :] = send_ref[
        pl.ds(pl.multiple_of(me * cap, cap), cap), :
    ]
    hubs_ref[pl.ds(pl.multiple_of(me * hub, hub), hub), :] = hub_ref[...]

    def put_dw(m, lhs_ref):
        for b in range(width // lanes):
            part = dot(lhs_ref[...], g_ref[:, lanes * b : lanes * (b + 1)], INNER)
            part = part.reshape(parts, 2, 8, lanes)
            for a in range(2):
                dw_ref[m, 4 * a + b] = part[:, a]

    def dw_copy(k, m):
        p = dp_peer(k)
        return pltpu.make_async_remote_copy(
            src_ref=dw_ref.at[m, p],
            dst_ref=dw_recv_ref.at[m, lane],
            send_sem=w_send.at[m, k],
            recv_sem=w_recv.at[m, k],
            device_id={"dp": p},
        )

    def dw_arrival(k, m):
        p = lax.rem(lane + groups - k, groups)
        spot = dw_recv_ref.at[m, p]
        return pltpu.make_async_remote_copy(
            src_ref=spot,
            dst_ref=spot,
            send_sem=w_send.at[m, k],
            recv_sem=w_recv.at[m, k],
            device_id={"dp": dp_peer(k)},
        )

    for k in range(slots):
        live_ref[k : k + 1, :] = jnp.where(
            deg_ref[...] > k, nbr_ref[k : k + 1, :], -1
        )
    for i in range(rows // lanes):
        inv_ref[lanes * i : lanes * (i + 1), :] = column(
            1.0 / deg_ref[:, lanes * i : lanes * (i + 1)].astype(F32)
        )
    tall = 32
    row_iota = lax.broadcasted_iota(jnp.int32, (tall, rows), 0)

    @pl.loop(0, height // tall)
    def _(i):
        total = jnp.zeros((tall, rows), F32)
        spot = row_iota + i * tall
        for k in range(slots):
            total = total + jnp.where(live_ref[k : k + 1, :] == spot, 1.0, 0.0)
        count_t_ref[pl.ds(pl.multiple_of(i * tall, tall), tall), :] = total.astype(BF16)

    step = 128

    @pl.loop(0, rows // step)
    def _(i):
        span = pl.ds(pl.multiple_of(i * step, step), step)
        inv = inv_ref[span, :]
        back = dot(g_ref[span, :], wn_ref[...], TRANS) * jnp.concatenate([inv] * 4, axis=1)
        hi = back.astype(BF16)
        hi_ref[span, :] = hi
        lo_ref[span, :] = (back - hi.astype(F32)).astype(BF16)

    def dtable(start):
        c = count_t_ref[pl.ds(pl.multiple_of(start, step), step), :]
        return dot(c, hi_ref[...]) + dot(c, lo_ref[...])

    @pl.loop(0, sent // step)
    def _(i):
        span = pl.ds(pl.multiple_of(i * step, step), step)
        back_send_ref[span, :] = dtable(2 * rows + i * step).astype(BF16)

    @pl.loop(0, rows // step)
    def _(i):
        span = pl.ds(pl.multiple_of(i * step, step), step)
        back_hub_ref[span, :] = dtable(rows + i * step).astype(BF16)

    @pl.loop(1, parts)
    def _(k):
        exchange(k, back_send_ref, back_recv_ref, b_send, b_recv, cap, False).start()
        exchange(k, back_hub_ref, back_hubs_ref, bh_send, bh_recv, hub, False).start()

    back_recv_ref[pl.ds(pl.multiple_of(me * cap, cap), cap), :] = back_send_ref[
        pl.ds(pl.multiple_of(me * cap, cap), cap), :
    ]
    back_hubs_ref[pl.ds(pl.multiple_of(me * hub, hub), hub), :] = back_hub_ref[
        pl.ds(pl.multiple_of(me * hub, hub), hub), :
    ]

    put_dw(0, own_ref)

    @pl.loop(1, groups)
    def _(k):
        dw_copy(k, 0).start()

    @pl.loop(0, rows // step)
    def _(i):
        span = pl.ds(pl.multiple_of(i * step, step), step)
        dlocal_ref[span, :] = dtable(i * step) + dot(g_ref[span, :], ws_ref[...], TRANS)
        base_ref[span, :] = dot(own_ref[span, :], ws_ref[...])

    for i in range(height // lanes):
        count_ref[:, lanes * i : lanes * (i + 1)] = jnp.transpose(
            count_t_ref[lanes * i : lanes * (i + 1), :]
        )

    down = lax.broadcasted_iota(jnp.int32, (rows, lanes), 0)
    for i in range(sent // lanes + 1):
        spread_ref[:, lanes * i : lanes * (i + 1)] = (
            (idx_ref[i : i + 1, :] == down).astype(F32).astype(BF16)
        )

    @pl.loop(1, parts)
    def _(k):
        arrival(k, recv_ref, f_send, f_recv, cap).wait_recv()
        arrival(k, hubs_ref, fh_send, fh_recv, hub).wait_recv()

    @pl.loop(0, rows // step)
    def _(i):
        span = pl.ds(pl.multiple_of(i * step, step), step)
        total = dot(count_ref[span, :rows], own_ref[...])
        total = total + dot(count_ref[span, rows : 2 * rows], hubs_ref[...])
        total = total + dot(count_ref[span, 2 * rows :], recv_ref[...])
        agg_ref[span, :] = (total * jnp.concatenate([inv_ref[span, :]] * 4, axis=1)).astype(BF16)

    put_dw(1, agg_ref)

    @pl.loop(1, groups)
    def _(k):
        dw_copy(k, 1).start()

    @pl.loop(0, rows // step)
    def _(i):
        span = pl.ds(pl.multiple_of(i * step, step), step)
        out_ref[span, :] = (base_ref[span, :] + dot(agg_ref[span, :], wn_ref[...])).astype(BF16)

    for m in range(2):

        @pl.loop(1, groups)
        def _(k):
            dw_arrival(k, m).wait_recv()

        dw_recv_ref[m, lane] = dw_ref[m, lane]

        @pl.loop(0, parts)
        def _(q):
            total = dw_recv_ref[m, 0, q]
            for p in range(1, groups):
                total = total + dw_recv_ref[m, p, q]
            slab_ref[q, m] = total

    def slab_copy(k):
        q = graph_peer(k)
        return pltpu.make_async_remote_copy(
            src_ref=slab_ref.at[q],
            dst_ref=slab_recv_ref.at[me],
            send_sem=s_send.at[k],
            recv_sem=s_recv.at[k],
            device_id={"graph": q},
        )

    def slab_arrival(k):
        spot = slab_recv_ref.at[lax.rem(me + parts - k, parts)]
        return pltpu.make_async_remote_copy(
            src_ref=spot,
            dst_ref=spot,
            send_sem=s_send.at[k],
            recv_sem=s_recv.at[k],
            device_id={"graph": graph_peer(k)},
        )

    @pl.loop(1, parts)
    def _(k):
        slab_copy(k).start()

    slab_recv_ref[me] = slab_ref[me]

    @pl.loop(1, parts)
    def _(k):
        arrival(k, back_recv_ref, b_send, b_recv, cap).wait_recv()
        arrival(k, back_hubs_ref, bh_send, bh_recv, hub).wait_recv()

    @pl.loop(0, rows // step)
    def _(i):
        span = pl.ds(pl.multiple_of(i * step, step), step)
        total = dlocal_ref[span, :] + dot(spread_ref[span, :sent], back_recv_ref[...])
        tail = spread_ref[span, sent:]
        for j in range(parts * hub // lanes):
            total = total + dot(tail, back_hubs_ref[lanes * j : lanes * (j + 1), :])
        gf_ref[span, :] = total.astype(BF16)

    @pl.loop(1, parts)
    def _(k):
        slab_arrival(k).wait_recv()

    for m in range(2):
        total = slab_recv_ref[0, m]
        for q in range(1, parts):
            total = total + slab_recv_ref[q, m]
        fin_ref[m] = total * scale

    def fin_copy(k):
        p = dp_peer(k)
        return pltpu.make_async_remote_copy(
            src_ref=fin_ref,
            dst_ref=fin_recv_ref.at[lane],
            send_sem=e_send.at[k],
            recv_sem=e_recv.at[k],
            device_id={"dp": p},
        )

    def fin_arrival(k):
        spot = fin_recv_ref.at[lax.rem(lane + groups - k, groups)]
        return pltpu.make_async_remote_copy(
            src_ref=spot,
            dst_ref=spot,
            send_sem=e_send.at[k],
            recv_sem=e_recv.at[k],
            device_id={"dp": dp_peer(k)},
        )

    @pl.loop(1, groups)
    def _(k):
        fin_copy(k).start()

    fin_recv_ref[lane] = fin_ref[...]

    @pl.loop(1, groups)
    def _(k):
        fin_arrival(k).wait_recv()

    for a in range(2):
        for b in range(width // lanes):
            here = (slice(8 * a, 8 * (a + 1)), slice(lanes * b, lanes * (b + 1)))
            gws_ref[here] = fin_recv_ref[4 * a + b, 0]
            gwn_ref[here] = fin_recv_ref[4 * a + b, 1]

    @pl.loop(1, parts)
    def _(k):
        exchange(k, send_ref, recv_ref, f_send, f_recv, cap, False).wait_send()
        exchange(k, hub_ref, hubs_ref, fh_send, fh_recv, hub, True).wait_send()
        exchange(k, back_send_ref, back_recv_ref, b_send, b_recv, cap, False).wait_send()
        exchange(k, back_hub_ref, back_hubs_ref, bh_send, bh_recv, hub, False).wait_send()
        slab_copy(k).wait_send()

    @pl.loop(1, groups)
    def _(k):
        dw_copy(k, 0).wait_send()
        dw_copy(k, 1).wait_send()
        fin_copy(k).wait_send()


def shards(feats, grad_out, w_self, w_neigh, nbr, deg, hub_rows, send_rows):
    own = feats[0]
    rows, width = own.shape
    slots = nbr.shape[2]
    parts = lax.axis_size("graph")
    groups = lax.axis_size("dp")
    hub = hub_rows.shape[1]
    cap = send_rows.shape[3]
    sent = parts * cap
    nhub = parts * hub
    height = rows + nhub + sent
    idx = jnp.concatenate(
        [send_rows.reshape(sent // 128, 128), jnp.tile(hub_rows, (1, 128 // hub))], axis=0
    )
    scale = float((groups * parts * rows) ** -0.5)
    vmem = pltpu.VMEM
    dma = pltpu.SemaphoreType.DMA
    outs = pl.pallas_call(
        functools.partial(layer_kernel, parts, groups, scale),
        out_shape=(
            jax.ShapeDtypeStruct((rows, width), BF16),
            jax.ShapeDtypeStruct((rows, width), BF16),
            jax.ShapeDtypeStruct((width // parts, width), F32),
            jax.ShapeDtypeStruct((width // parts, width), F32),
        ),
        in_specs=[pl.BlockSpec(memory_space=vmem)] * 7,
        out_specs=[pl.BlockSpec(memory_space=vmem)] * 4,
        scratch_shapes=[
            vmem((slots, rows), jnp.int32),
            vmem((sent + hub, rows), BF16),
            vmem((rows, sent + 128), BF16),
            vmem((height, rows), BF16),
            vmem((rows, height), BF16),
            vmem((sent, width), BF16),
            vmem((hub, width), BF16),
            vmem((sent, width), BF16),
            vmem((nhub, width), BF16),
            vmem((rows, width), BF16),
            vmem((rows, width), BF16),
            vmem((rows, width), F32),
            vmem((sent, width), BF16),
            vmem((nhub, width), BF16),
            vmem((sent, width), BF16),
            vmem((nhub, width), BF16),
            vmem((rows, width), F32),
            vmem((rows, width), BF16),
            vmem((rows, 128), F32),
            vmem((2, groups, parts, 8, 128), F32),
            vmem((2, groups, parts, 8, 128), F32),
            vmem((parts, 2, 8, 128), F32),
            vmem((parts, 2, 8, 128), F32),
            vmem((2, 8, 128), F32),
            vmem((groups, 2, 8, 128), F32),
        ]
        + [dma((parts,))] * 8
        + [dma((2, groups))] * 2
        + [dma((parts,))] * 2
        + [dma((groups,))] * 2,
        compiler_params=pltpu.CompilerParams(collective_id=0, has_side_effects=True),
    )(own, grad_out[0], w_self, w_neigh, nbr[0].T, deg, idx)
    out, grad_feats, grad_w_self, grad_w_neigh = outs
    return (out[None], grad_feats[None], grad_w_self, grad_w_neigh)


def solution(mesh):
    placed = (
        P("dp", "graph", None),
        P("dp", "graph", None),
        P(),
        P(),
        P("dp", "graph", None),
        P("dp", "graph"),
        P("dp", "graph"),
        P("dp", "graph", None, None),
    )
    return jax.shard_map(
        shards,
        mesh=mesh,
        in_specs=placed,
        out_specs=(
            P("dp", "graph", None),
            P("dp", "graph", None),
            P("graph", None),
            P("graph", None),
        ),
        check_vma=False,
    )
```

time: 490 us -> 105 us (0.21); the launches traced: 481 us -> 104 us
  waiting for transfers between devices: 263 us -> 0 us
  Pallas kernels: 0 us -> 96.8 us
  other arithmetic: 95.4 us -> 0.61 us
  blocking collectives: 43.9 us -> 0 us
  local copies, waits for them, and re-layouts: 35.2 us -> 6.25 us
  starting transfers between devices: 18.4 us -> 0 us
  between operations: 16.3 us -> 0.66 us
  matrix products: 9.02 us -> 0 us
    psum x1 -> x0, waiting for transfers between devices: 138 us -> none  [shards(): sum_self, sum_neigh = lax.psum((dws, dwn), ('dp', 'graph'))]
    reduce_scatter x1 -> x0, waiting for transfers between devices: 125 us -> none  [shards(): lax.psum_scatter(dtable[rows:rows + nhub].astype(jnp.bfloat16), 'graph',...]
    pallas_call x0 -> x1, Pallas kernels: none -> 96.8 us  [shards(): pl.pallas_call(functools.partial(layer_kernel, parts, groups, scale), out...]
    scatter-add x12 -> x0, other arithmetic: 84 us -> none  [the longest x10 74.8 us: shards(): dtable = dtable.at[target].add(back, mode='drop')]
    all_gather x1 -> x0, blocking collectives: 43.9 us -> none  [shards(): hubs = lax.all_gather(hub_local, 'graph', axis=0, tiled=True)]
    gather x12 -> x0, local copies, waits for them, and re-layouts: 33.1 us -> none  [the longest x10 26.2 us: shards(): table[idx[:, k]].astype(jnp.float32)]
    all_to_all x2 -> x0, starting transfers between devices: 18 us -> none  [the longest x1 12.2 us: shards(): lax.all_to_all(outgoing, 'graph', split_axis=0, concat_axis=0, tiled=True)]
    dot_general x6 -> x0, matrix products: 9.02 us -> none  [the longest x1 2.46 us: shards(): jnp.dot(agg, w_neigh, preferred_element_type=jnp.float32)]
  transfers between devices with their start and end apart: 4 -> 0, of which waited for: 2 -> 0; matrix products, arithmetic and copies ran while one was open for 27% -> 0% of each run, Pallas kernels for 0% -> 0%
where the time goes in v1:
time: 105 us; the launch traced here: 104 us
  Pallas kernels  96.8 us (92%)
  local copies, waits for them, and re-layouts  6.25 us (6%)
    pallas_call x1, Pallas kernels, shards(): pl.pallas_call(functools.partial(layer_kernel, parts, groups, scale), out...  96.8 us
    unnamed x15, local copies, waits for them, and re-layouts  5.38 us

profile of v1, /device:TPU:1, one launch (start us, length us, event | category | flops | bytes accessed | tf_op | source)
XLA Modules:
  0.0 104.3 jit_solution(1022968163531612281)
XLA Ops:
  0.6 0.0 copy-start.4
  0.6 0.6 copy-done.4
  1.3 0.0 copy-start.3
  1.3 0.1 tile.13
  1.4 0.8 reshape.17
  2.2 0.6 pad_add_fusion.idx_ref
  2.8 0.0 copy-done.3
  2.8 0.6 copy.14
  3.4 96.8 %shard_map.111 = (bf16[512,512]{1,0:T(8,128)(2,1)}, bf16[512,512]{1,0:T(8,128)(2,1)}, f32[16,512]{1,0:T(8,128)}, f32[16,512]{1,0:T(8,128)}) custom-call(bf16[512,512]{1,0:T(8,128)(2,1)} %bitcast.12, bf16[512,512]{1,0:T(8,128)(2,1)} %bitcast.13, bf16[512,512]{1,0:T(8,128)(2,1)} %ws_ref.1, bf16[512,512]{1,0:T(8,128)(2,1)} %wn_ref.1, s32[10,512]{1,0:T(8,128)} %bitcast.16, ...), custom_call_target="tpu_custom_call" | custom-call | tf_op jit(solution)/shard_map/pallas_call | solution.py:414
  100.2 0.0 copy-start
  100.2 1.9 %copy.19 = bf16[1,512,512]{2,1,0:T(8,128)(2,1)} copy(bf16[1,512,512]{2,1,0:T(8,128)(2,1)} %bitcast.15) | data formatting | bytes 1048576
  102.1 0.0 copy-done
  102.1 0.0 copy-start.2
  102.1 0.8 copy.20
  102.9 0.0 copy-done.2
  102.9 0.0 copy-start.1
  102.9 0.6 copy.21
  103.5 0.2 copy-done.1
  103.7 0.6 copy.22
  (1 shorter events, 0.0 us)
Async XLA Ops:
  0.6 0.7 copy-start.4
  1.3 1.5 %copy-start.3 = (s32[1,512,10]{1,0,2:T(1,128)S(1)}, s32[1,512,10]{1,0,2:T(1,128)}, u32[]{:S(2)}) copy-start(s32[1,512,10]{1,0,2:T(1,128)} %param.12) | copy-start | bytes 61444
  100.2 1.9 %copy-start = (bf16[512,512]{1,0:T(8,128)(2,1)S(1)}, bf16[512,512]{1,0:T(8,128)(2,1)}, u32[]{:S(2)}) copy-start(bf16[512,512]{1,0:T(8,128)(2,1)} %get-tuple-element.9) | copy-start | bytes 1572868
  102.1 0.8 copy-start.2
  102.9 0.8 copy-start.1

commit v2 on v1

v2 whole, which is shorter than its diff:
```python
import functools

import jax
import jax.numpy as jnp
from jax import lax
from jax.experimental import pallas as pl
from jax.experimental.pallas import tpu as pltpu
from jax.sharding import PartitionSpec as P

F32 = jnp.float32
BF16 = jnp.bfloat16
COLUMNS = 4
TRANS = (((1,), (1,)), ((), ()))


def dot(a, b, dims=(((1,), (0,)), ((), ()))):
    return lax.dot_general(a, b, dims, preferred_element_type=F32)


def layer_kernel(
    parts,
    groups,
    scale,
    own_ref,
    g_ref,
    ws_ref,
    wn_ref,
    nbr_ref,
    deg_ref,
    rows_ref,
    hub_rows_ref,
    out_ref,
    gf_ref,
    gws_ref,
    gwn_ref,
    idx_ref,
    live_ref,
    pick_ref,
    spread_ref,
    count_t_ref,
    count_ref,
    send_ref,
    hub_ref,
    recv_ref,
    hubs_ref,
    hi_ref,
    lo_ref,
    grad_ref,
    back_send_ref,
    back_hub_ref,
    back_recv_ref,
    back_slab_ref,
    back_sum_ref,
    back_hubs_ref,
    base_ref,
    total_ref,
    agg_ref,
    inv_ref,
    dw_ref,
    dw_recv_ref,
    slab_ref,
    slab_recv_ref,
    ring_ref,
    ring_recv_ref,
    fin_ref,
    fin_recv_ref,
    f_send,
    f_recv,
    b_send,
    b_recv,
    hz_send,
    hz_recv,
    hy_send,
    hy_recv,
    ty_send,
    ty_recv,
    tz_send,
    tz_recv,
    w_send,
    w_recv,
    sy_send,
    sy_recv,
    sz_send,
    sz_recv,
    e_send,
    e_recv,
):
    rows, width = own_ref.shape
    slots = nbr_ref.shape[0]
    cap = recv_ref.shape[0] // parts
    hub = hub_ref.shape[0]
    sent = recv_ref.shape[0]
    nhub = hubs_ref.shape[0]
    height = count_t_ref.shape[0]
    ny = COLUMNS
    nz = parts // ny
    lanes = 128
    step = 128
    me = lax.axis_index("graph")
    lane = lax.axis_index("dp")
    z, y = me // ny, lax.rem(me, ny)

    def at(base, size):
        return pl.ds(pl.multiple_of(base * size, size), size)

    def peer(k, sign=1):
        dz, dy = k // ny, lax.rem(k, ny)
        return lax.rem(z + nz + sign * dz, nz) * ny + lax.rem(y + ny + sign * dy, ny)

    def z_at(k):
        return lax.rem(z + k + nz, nz)

    def y_at(k):
        return lax.rem(y + k + ny, ny)

    def d_at(k):
        return lax.rem(lane + k + groups, groups)

    def remote(src, dst, ssem, rsem, device):
        return pltpu.make_async_remote_copy(
            src_ref=src, dst_ref=dst, send_sem=ssem, recv_sem=rsem, device_id=device
        )

    def to_z(k, src, dst, ssem, rsem):
        return remote(src, dst, ssem.at[k], rsem.at[k], {"graph": z_at(k) * ny + y})

    def to_y(k, src, dst, ssem, rsem):
        return remote(src, dst, ssem.at[k], rsem.at[k], {"graph": z * ny + y_at(k)})

    def to_all(k, src, dst, ssem, rsem):
        return remote(src, dst, ssem.at[k], rsem.at[k], {"graph": peer(k)})

    barrier = pltpu.get_barrier_semaphore()

    @pl.loop(1, parts)
    def _(k):
        pl.semaphore_signal(barrier, inc=1, device_id={"graph": peer(k)})

    @pl.loop(1, groups)
    def _(k):
        pl.semaphore_signal(barrier, inc=1, device_id={"dp": d_at(k)})

    per = lanes // cap
    for i in range(sent // lanes):
        idx_ref[i : i + 1, :] = jnp.concatenate(
            [rows_ref[per * i + c : per * i + c + 1, :] for c in range(per)], axis=1
        )
    last = sent // lanes
    idx_ref[last : last + 1, :] = jnp.concatenate([hub_rows_ref[...]] * (lanes // hub), axis=1)

    def column(row):
        return jnp.transpose(jnp.broadcast_to(row, (lanes, lanes)))

    lane_iota = lax.broadcasted_iota(jnp.int32, (lanes, lanes), 1)
    for i in (last, *range(last)):
        spot = column(idx_ref[i : i + 1, :])
        tall = lanes if i < last else hub
        for j in range(width // lanes):
            hit = (spot == lane_iota + lanes * j).astype(F32).astype(BF16)
            pick_ref[lanes * i : lanes * i + tall, lanes * j : lanes * (j + 1)] = hit[:tall]
    hub_ref[...] = dot(pick_ref[sent : sent + hub, :], own_ref[...]).astype(BF16)
    hubs_ref[at(y * nz + z, hub), :] = hub_ref[...]
    for i in range(sent // 256):
        send_ref[256 * i : 256 * (i + 1), :] = dot(
            pick_ref[256 * i : 256 * (i + 1), :], own_ref[...]
        ).astype(BF16)

    pl.semaphore_wait(barrier, parts - 1 + groups - 1)

    def hub_z(k):
        return to_z(k, hub_ref, hubs_ref.at[at(y * nz + z, hub)], hz_send, hz_recv)

    def hub_z_in(k):
        spot = hubs_ref.at[at(y * nz + z_at(-k), hub)]
        return to_z(k, spot, spot, hz_send, hz_recv)

    def hub_y(k):
        spot = hubs_ref.at[at(y, nz * hub)]
        return to_y(k, spot, spot, hy_send, hy_recv)

    def hub_y_in(k):
        spot = hubs_ref.at[at(y_at(-k), nz * hub)]
        return to_y(k, spot, spot, hy_send, hy_recv)

    def forth(k):
        return to_all(
            k, send_ref.at[at(peer(k), cap)], recv_ref.at[at(me, cap)], f_send, f_recv
        )

    def forth_in(k):
        spot = recv_ref.at[at(peer(k, -1), cap)]
        return to_all(k, spot, spot, f_send, f_recv)

    def back(k):
        return to_all(
            k, back_send_ref.at[at(peer(k), cap)], back_recv_ref.at[at(me, cap)], b_send, b_recv
        )

    def back_in(k):
        spot = back_recv_ref.at[at(peer(k, -1), cap)]
        return to_all(k, spot, spot, b_send, b_recv)

    @pl.loop(1, nz)
    def _(k):
        hub_z(k).start()

    @pl.loop(1, parts)
    def _(k):
        forth(k).start()

    recv_ref[at(me, cap), :] = send_ref[at(me, cap), :]

    for k in range(slots):
        name = nbr_ref[k]
        h = name - rows
        moved = rows + ((h // hub) % ny) * (nz * hub) + (h // (hub * ny)) * hub + h % hub
        name = jnp.where((h >= 0) & (h < nhub), moved, name)
        live_ref[k : k + 1, :] = jnp.where(deg_ref[...] > k, name, -1)
    for i in range(rows // lanes):
        inv_ref[lanes * i : lanes * (i + 1), :] = column(
            1.0 / deg_ref[:, lanes * i : lanes * (i + 1)].astype(F32)
        )
    tall = 32
    row_iota = lax.broadcasted_iota(jnp.int32, (tall, rows), 0)

    @pl.loop(0, height // tall)
    def _(i):
        total = jnp.zeros((tall, rows), F32)
        spot = row_iota + i * tall
        for k in range(slots):
            total = total + jnp.where(live_ref[k : k + 1, :] == spot, 1.0, 0.0)
        count_t_ref[at(i, tall), :] = total.astype(BF16)

    @pl.loop(1, nz)
    def _(k):
        hub_z_in(k).wait_recv()

    @pl.loop(1, ny)
    def _(k):
        hub_y(k).start()

    def by_vertex(span):
        return jnp.concatenate([inv_ref[span, :]] * (width // lanes), axis=1)

    @pl.loop(0, rows // step)
    def _(i):
        span = at(i, step)
        term = dot(g_ref[span, :], wn_ref[...], TRANS) * by_vertex(span)
        hi = term.astype(BF16)
        hi_ref[span, :] = hi
        lo_ref[span, :] = (term - hi.astype(F32)).astype(BF16)

    def dtable(start):
        c = count_t_ref[pl.ds(pl.multiple_of(start, step), step), :]
        return dot(c, hi_ref[...]) + dot(c, lo_ref[...])

    @pl.loop(0, nhub // step)
    def _(i):
        back_hub_ref[at(i, step), :] = dtable(rows + i * step).astype(BF16)

    def term_y(k):
        return to_y(
            k, back_hub_ref.at[at(y_at(k), nz * hub)], back_slab_ref.at[y], ty_send, ty_recv
        )

    def term_y_in(k):
        spot = back_slab_ref.at[y_at(-k)]
        return to_y(k, spot, spot, ty_send, ty_recv)

    def term_z(k):
        return to_z(
            k, back_sum_ref.at[at(z_at(k), hub)], back_hubs_ref.at[at(z, hub)], tz_send, tz_recv
        )

    def term_z_in(k):
        spot = back_hubs_ref.at[at(z_at(-k), hub)]
        return to_z(k, spot, spot, tz_send, tz_recv)

    @pl.loop(1, ny)
    def _(k):
        term_y(k).start()

    @pl.loop(0, sent // step)
    def _(i):
        back_send_ref[at(i, step), :] = dtable(rows + nhub + i * step).astype(BF16)

    @pl.loop(1, parts)
    def _(k):
        back(k).start()

    back_recv_ref[at(me, cap), :] = back_send_ref[at(me, cap), :]
    back_slab_ref[y] = back_hub_ref[at(y, nz * hub), :]

    def put_dw(m, lhs_ref):
        own16 = step // 16

        @pl.loop(0, width // step)
        def _(i):
            lhs = jnp.transpose(lhs_ref[:, at(i, step)])
            part = dot(lhs, g_ref[...]).reshape(own16, 2, 8, width)
            for b in range(width // lanes):
                for a in range(2):
                    dw_ref[m, 4 * a + b, at(i, own16)] = part[
                        :, a, :, lanes * b : lanes * (b + 1)
                    ]

    def dw_copy(k, m):
        p = d_at(k)
        return remote(
            dw_ref.at[m, p], dw_recv_ref.at[m, lane], w_send.at[m, k], w_recv.at[m, k], {"dp": p}
        )

    def dw_in(k, m):
        spot = dw_recv_ref.at[m, d_at(-k)]
        return remote(spot, spot, w_send.at[m, k], w_recv.at[m, k], {"dp": d_at(k)})

    put_dw(0, own_ref)

    @pl.loop(1, groups)
    def _(k):
        dw_copy(k, 0).start()

    @pl.loop(1, ny)
    def _(k):
        term_y_in(k).wait_recv()

    total = back_slab_ref[0].astype(F32)
    for k in range(1, ny):
        total = total + back_slab_ref[k].astype(F32)
    back_sum_ref[...] = total.astype(BF16)

    @pl.loop(1, nz)
    def _(k):
        term_z(k).start()

    back_hubs_ref[at(z, hub), :] = back_sum_ref[at(z, hub), :]

    for i in range(height // lanes):
        count_ref[:, lanes * i : lanes * (i + 1)] = jnp.transpose(
            count_t_ref[lanes * i : lanes * (i + 1), :]
        )

    @pl.loop(0, rows // step)
    def _(i):
        span = at(i, step)
        grad_ref[span, :] = dtable(i * step) + dot(g_ref[span, :], ws_ref[...], TRANS)
        base_ref[span, :] = dot(own_ref[span, :], ws_ref[...])
        total_ref[span, :] = dot(count_ref[span, :rows], own_ref[...])

    down = lax.broadcasted_iota(jnp.int32, (rows, lanes), 0)
    for i in range(last + 1):
        spread_ref[:, lanes * i : lanes * (i + 1)] = (
            (idx_ref[i : i + 1, :] == down).astype(F32).astype(BF16)
        )

    @pl.loop(1, ny)
    def _(k):
        hub_y_in(k).wait_recv()

    @pl.loop(0, rows // step)
    def _(i):
        span = at(i, step)
        total_ref[span, :] += dot(count_ref[span, rows : rows + nhub], hubs_ref[...])

    near = [0]
    for k in range(1, nz // 2):
        near += [k, nz - k]
    near.append(nz // 2)
    plane = ny * cap
    for dz in near:

        @pl.loop(max(dz * ny, 1), (dz + 1) * ny)
        def _(k):
            forth_in(k).wait_recv()

        src = z_at(-dz)

        @pl.loop(0, rows // step)
        def _(i):
            span = at(i, step)
            c = count_ref[span, pl.ds(pl.multiple_of(rows + nhub + src * plane, plane), plane)]
            total = total_ref[span, :] + dot(c, recv_ref[at(src, plane), :])
            if dz != near[-1]:
                total_ref[span, :] = total
            else:
                agg_ref[span, :] = (total * by_vertex(span)).astype(BF16)

    put_dw(1, agg_ref)

    @pl.loop(1, groups)
    def _(k):
        dw_copy(k, 1).start()

    @pl.loop(0, rows // step)
    def _(i):
        span = at(i, step)
        out_ref[span, :] = (base_ref[span, :] + dot(agg_ref[span, :], wn_ref[...])).astype(BF16)

    for m in range(2):

        @pl.loop(1, groups)
        def _(k):
            dw_in(k, m).wait_recv()

        dw_recv_ref[m, lane] = dw_ref[m, lane]

        @pl.loop(0, parts)
        def _(q):
            total = dw_recv_ref[m, 0, q]
            for p in range(1, groups):
                total = total + dw_recv_ref[m, p, q]
            slab_ref[lax.rem(q, ny), q // ny, m] = total

    def slab_y(k):
        return to_y(k, slab_ref.at[y_at(k)], slab_recv_ref.at[y], sy_send, sy_recv)

    def slab_y_in(k):
        spot = slab_recv_ref.at[y_at(-k)]
        return to_y(k, spot, spot, sy_send, sy_recv)

    def ring(k):
        return to_z(k, ring_ref.at[z_at(k)], ring_recv_ref.at[z], sz_send, sz_recv)

    def ring_in(k):
        spot = ring_recv_ref.at[z_at(-k)]
        return to_z(k, spot, spot, sz_send, sz_recv)

    @pl.loop(1, ny)
    def _(k):
        slab_y(k).start()

    slab_recv_ref[y] = slab_ref[y]

    @pl.loop(1, ny)
    def _(k):
        slab_y_in(k).wait_recv()

    @pl.loop(0, nz)
    def _(q):
        total = slab_recv_ref[0, q]
        for p in range(1, ny):
            total = total + slab_recv_ref[p, q]
        ring_ref[q] = total

    @pl.loop(1, nz)
    def _(k):
        ring(k).start()

    ring_recv_ref[z] = ring_ref[z]

    @pl.loop(1, nz)
    def _(k):
        term_z_in(k).wait_recv()

    @pl.loop(0, rows // step)
    def _(i):
        span = at(i, step)
        grad_ref[span, :] += dot(spread_ref[span, sent:], back_hubs_ref[...])

    def finish_weights():
        @pl.loop(1, nz)
        def _(k):
            ring_in(k).wait_recv()

        total = ring_recv_ref[0]
        for q in range(1, nz):
            total = total + ring_recv_ref[q]
        fin_ref[...] = total * scale
        fin_recv_ref[lane] = fin_ref[...]

        @pl.loop(1, groups)
        def _(k):
            fin(k).start()

    def fin(k):
        return remote(
            fin_ref, fin_recv_ref.at[lane], e_send.at[k], e_recv.at[k], {"dp": d_at(k)}
        )

    def fin_in(k):
        spot = fin_recv_ref.at[d_at(-k)]
        return remote(spot, spot, e_send.at[k], e_recv.at[k], {"dp": d_at(k)})

    for dz in near:

        @pl.loop(max(dz * ny, 1), (dz + 1) * ny)
        def _(k):
            back_in(k).wait_recv()

        if dz == near[-1]:
            finish_weights()
        src = z_at(-dz)

        @pl.loop(0, rows // step)
        def _(i):
            span = at(i, step)
            c = spread_ref[span, at(src, plane)]
            total = grad_ref[span, :] + dot(c, back_recv_ref[at(src, plane), :])
            if dz != near[-1]:
                grad_ref[span, :] = total
            else:
                gf_ref[span, :] = total.astype(BF16)

    @pl.loop(1, groups)
    def _(k):
        fin_in(k).wait_recv()

    for a in range(2):
        for b in range(width // lanes):
            here = (slice(8 * a, 8 * (a + 1)), slice(lanes * b, lanes * (b + 1)))
            gws_ref[here] = fin_recv_ref[4 * a + b, 0]
            gwn_ref[here] = fin_recv_ref[4 * a + b, 1]

    @pl.loop(1, parts)
    def _(k):
        forth(k).wait_send()
        back(k).wait_send()

    @pl.loop(1, nz)
    def _(k):
        hub_z(k).wait_send()
        term_z(k).wait_send()
        ring(k).wait_send()

    @pl.loop(1, ny)
    def _(k):
        hub_y(k).wait_send()
        term_y(k).wait_send()
        slab_y(k).wait_send()

    @pl.loop(1, groups)
    def _(k):
        dw_copy(k, 0).wait_send()
        dw_copy(k, 1).wait_send()
        fin(k).wait_send()


def shards(feats, grad_out, w_self, w_neigh, nbr, deg, hub_rows, send_rows):
    own = feats[0]
    rows, width = own.shape
    slots = nbr.shape[2]
    parts = lax.axis_size("graph")
    groups = lax.axis_size("dp")
    hub = hub_rows.shape[1]
    cap = send_rows.shape[3]
    sent = parts * cap
    nhub = parts * hub
    height = rows + nhub + sent
    ny = COLUMNS
    nz = parts // ny
    scale = float((groups * parts * rows) ** -0.5)
    vmem = pltpu.VMEM
    dma = pltpu.SemaphoreType.DMA
    outs = pl.pallas_call(
        functools.partial(layer_kernel, parts, groups, scale),
        out_shape=(
            jax.ShapeDtypeStruct((rows, width), BF16),
            jax.ShapeDtypeStruct((rows, width), BF16),
            jax.ShapeDtypeStruct((width // parts, width), F32),
            jax.ShapeDtypeStruct((width // parts, width), F32),
        ),
        in_specs=[pl.BlockSpec(memory_space=vmem)] * 8,
        out_specs=[pl.BlockSpec(memory_space=vmem)] * 4,
        scratch_shapes=[
            vmem((sent // 128 + 1, 128), jnp.int32),
            vmem((slots, rows), jnp.int32),
            vmem((sent + hub, rows), BF16),
            vmem((rows, sent + 128), BF16),
            vmem((height, rows), BF16),
            vmem((rows, height), BF16),
            vmem((sent, width), BF16),
            vmem((hub, width), BF16),
            vmem((sent, width), BF16),
            vmem((nhub, width), BF16),
            vmem((rows, width), BF16),
            vmem((rows, width), BF16),
            vmem((rows, width), F32),
            vmem((sent, width), BF16),
            vmem((nhub, width), BF16),
            vmem((sent, width), BF16),
            vmem((ny, nz * hub, width), BF16),
            vmem((nz * hub, width), BF16),
            vmem((nz * hub, width), BF16),
            vmem((rows, width), F32),
            vmem((rows, width), F32),
            vmem((rows, width), BF16),
            vmem((rows, 128), F32),
            vmem((2, groups, parts, 8, 128), F32),
            vmem((2, groups, parts, 8, 128), F32),
            vmem((ny, nz, 2, 8, 128), F32),
            vmem((ny, nz, 2, 8, 128), F32),
            vmem((nz, 2, 8, 128), F32),
            vmem((nz, 2, 8, 128), F32),
            vmem((2, 8, 128), F32),
            vmem((groups, 2, 8, 128), F32),
        ]
        + [dma((parts,))] * 4
        + ([dma((nz,))] * 2 + [dma((ny,))] * 2)
        + ([dma((ny,))] * 2 + [dma((nz,))] * 2)
        + [dma((2, groups))] * 2
        + ([dma((ny,))] * 2 + [dma((nz,))] * 2)
        + [dma((groups,))] * 2,
        compiler_params=pltpu.CompilerParams(collective_id=0, has_side_effects=True),
    )(
        own,
        grad_out[0],
        w_self,
        w_neigh,
        jnp.transpose(nbr, (2, 0, 1)),
        deg,
        send_rows[0, 0],
        hub_rows,
    )
    out, grad_feats, grad_w_self, grad_w_neigh = outs
    return (out[None], grad_feats[None], grad_w_self, grad_w_neigh)


def solution(mesh):
    placed = (
        P("dp", "graph", None),
        P("dp", "graph", None),
        P(),
        P(),
        P("dp", "graph", None),
        P("dp", "graph"),
        P("dp", "graph"),
        P("dp", "graph", None, None),
    )
    return jax.shard_map(
        shards,
        mesh=mesh,
        in_specs=placed,
        out_specs=(
            P("dp", "graph", None),
            P("dp", "graph", None),
            P("graph", None),
            P("graph", None),
        ),
        check_vma=False,
    )
```

time: 105 us -> 85.7 us (0.82)
  Pallas kernels: 96.8 us -> 80.8 us
  local copies, waits for them, and re-layouts: 6.25 us -> 4.11 us
    pallas_call x1, Pallas kernels: 96.8 us -> 80.8 us  [shards(): pl.pallas_call(functools.partial(layer_kernel, parts, groups, scale), out...]
    unnamed x15 -> x10, local copies, waits for them, and re-layouts: 5.38 us -> 4.11 us
where the time goes in v2:
time: 85.7 us; the launch traced here: 85.5 us
  Pallas kernels  80.8 us (94%)
  local copies, waits for them, and re-layouts  4.11 us (5%)
    pallas_call x1, Pallas kernels, shards(): pl.pallas_call(functools.partial(layer_kernel, parts, groups, scale), out...  80.8 us
    unnamed x10, local copies, waits for them, and re-layouts  4.11 us

profile of v2, /device:TPU:1, one launch (start us, length us, event | category | flops | bytes accessed | tf_op | source)
XLA Modules:
  0.0 85.5 jit_solution(10940973604811193538)
XLA Ops:
  0.6 80.8 %shard_map.111 = (bf16[512,512]{1,0:T(8,128)(2,1)}, bf16[512,512]{1,0:T(8,128)(2,1)}, f32[16,512]{1,0:T(8,128)}, f32[16,512]{1,0:T(8,128)}) custom-call(bf16[512,512]{1,0:T(8,128)(2,1)} %bitcast.8, bf16[512,512]{1,0:T(8,128)(2,1)} %bitcast.9, bf16[512,512]{1,0:T(8,128)(2,1)} %ws_ref.1, bf16[512,512]{1,0:T(8,128)(2,1)} %wn_ref.1, s32[10,1,512]{2,1,0:T(1,128)} %bitcast.10, ...), custom_call_target="tpu_custom_call" | custom-call | tf_op jit(solution)/shard_map/pallas_call | solution.py:554
  81.4 0.0 copy-start
  81.4 1.9 %copy.16 = bf16[1,512,512]{2,1,0:T(8,128)(2,1)} copy(bf16[1,512,512]{2,1,0:T(8,128)(2,1)} %bitcast.7) | data formatting | bytes 1048576
  83.3 0.0 copy-done
  83.3 0.0 copy-start.2
  83.3 0.8 copy.17
  84.1 0.0 copy-done.2
  84.1 0.0 copy-start.1
  84.1 0.6 copy.18
  84.8 0.2 copy-done.1
  84.9 0.6 copy.19
Async XLA Ops:
  81.4 1.9 %copy-start = (bf16[512,512]{1,0:T(8,128)(2,1)S(1)}, bf16[512,512]{1,0:T(8,128)(2,1)}, u32[]{:S(2)}) copy-start(bf16[512,512]{1,0:T(8,128)(2,1)} %get-tuple-element.9) | copy-start | bytes 1572868
  83.3 0.8 copy-start.2
  84.1 0.8 copy-start.1

commit v3 on v2

--- a/solution.py
+++ b/solution.py
@@ -21,6 +21,18 @@
     parts,
     groups,
     scale,
+    own_hbm,
+    g_hbm,
+    ws_hbm,
+    wn_hbm,
+    nbr_hbm,
+    deg_hbm,
+    rows_hbm,
+    hub_rows_hbm,
+    out_ref,
+    gf_ref,
+    gws_ref,
+    gwn_ref,
     own_ref,
     g_ref,
     ws_ref,
@@ -29,10 +41,6 @@
     deg_ref,
     rows_ref,
     hub_rows_ref,
-    out_ref,
-    gf_ref,
-    gws_ref,
-    gwn_ref,
     idx_ref,
     live_ref,
     pick_ref,
@@ -57,6 +65,7 @@
     agg_ref,
     inv_ref,
     dw_ref,
+    pair_ref,
     dw_recv_ref,
     slab_ref,
     slab_recv_ref,
@@ -64,6 +73,7 @@
     ring_recv_ref,
     fin_ref,
     fin_recv_ref,
+    load,
     f_send,
     f_recv,
     b_send,
@@ -76,6 +86,8 @@
     ty_recv,
     tz_send,
     tz_recv,
+    p_send,
+    p_recv,
     w_send,
     w_recv,
     sy_send,
@@ -95,7 +107,7 @@
     ny = COLUMNS
     nz = parts // ny
     lanes = 128
-    step = 128
+    step = 256
     me = lax.axis_index("graph")
     lane = lax.axis_index("dp")
     z, y = me // ny, lax.rem(me, ny)
@@ -139,6 +151,24 @@
     @pl.loop(1, groups)
     def _(k):
         pl.semaphore_signal(barrier, inc=1, device_id={"dp": d_at(k)})
+
+    wanted = (
+        (rows_hbm, rows_ref),
+        (hub_rows_hbm, hub_rows_ref),
+        (own_hbm, own_ref),
+        (nbr_hbm, nbr_ref),
+        (deg_hbm, deg_ref),
+        (g_hbm, g_ref),
+        (wn_hbm, wn_ref),
+        (ws_hbm, ws_ref),
+    )
+    loads = [
+        pltpu.make_async_copy(src, dst, load.at[i]) for i, (src, dst) in enumerate(wanted)
+    ]
+    for copy in loads:
+        copy.start()
+    for copy in loads[:3]:
+        copy.wait()
 
     per = lanes // cap
     for i in range(sent // lanes):
@@ -210,6 +240,9 @@
 
     recv_ref[at(me, cap), :] = send_ref[at(me, cap), :]
 
+    for copy in loads[3:]:
+        copy.wait()
+
     for k in range(slots):
         name = nbr_ref[k]
         h = name - rows
@@ -292,33 +325,65 @@
     back_slab_ref[y] = back_hub_ref[at(y, nz * hub), :]
 
     def put_dw(m, lhs_ref):
-        own16 = step // 16
-
-        @pl.loop(0, width // step)
+        own16 = lanes // 16
+
+        @pl.loop(0, width // lanes)
         def _(i):
-            lhs = jnp.transpose(lhs_ref[:, at(i, step)])
+            lhs = jnp.transpose(lhs_ref[:, at(i, lanes)])
             part = dot(lhs, g_ref[...]).reshape(own16, 2, 8, width)
             for b in range(width // lanes):
                 for a in range(2):
-                    dw_ref[m, 4 * a + b, at(i, own16)] = part[
+                    dest = 4 * a + b
+                    dw_ref[m, dest % 2, dest // 2, at(i, own16)] = part[
                         :, a, :, lanes * b : lanes * (b + 1)
                     ]
 
+    nx = groups // 2
+    core = lax.rem(lane, 2)
+    x = lane // 2
+
+    def x_at(k):
+        return lax.rem(x + k + nx, nx)
+
+    def pair(m):
+        return remote(
+            dw_ref.at[m, 1 - core],
+            pair_ref.at[m],
+            p_send.at[m],
+            p_recv.at[m],
+            {"dp": 2 * x + 1 - core},
+        )
+
+    def pair_sum(m):
+        pair(m).wait_recv()
+
+        @pl.loop(0, nx)
+        def _(q):
+            pair_ref[m, q] += dw_ref[m, core, q]
+
+        @pl.loop(1, nx)
+        def _(k):
+            dw_copy(k, m).start()
+
+        dw_recv_ref[m, x] = pair_ref[m, x]
+
     def dw_copy(k, m):
-        p = d_at(k)
         return remote(
-            dw_ref.at[m, p], dw_recv_ref.at[m, lane], w_send.at[m, k], w_recv.at[m, k], {"dp": p}
+            pair_ref.at[m, x_at(k)],
+            dw_recv_ref.at[m, x],
+            w_send.at[m, k],
+            w_recv.at[m, k],
+            {"dp": 2 * x_at(k) + core},
         )
 
     def dw_in(k, m):
-        spot = dw_recv_ref.at[m, d_at(-k)]
-        return remote(spot, spot, w_send.at[m, k], w_recv.at[m, k], {"dp": d_at(k)})
+        spot = dw_recv_ref.at[m, x_at(-k)]
+        return remote(
+            spot, spot, w_send.at[m, k], w_recv.at[m, k], {"dp": 2 * x_at(k) + core}
+        )
 
     put_dw(0, own_ref)
-
-    @pl.loop(1, groups)
-    def _(k):
-        dw_copy(k, 0).start()
+    pair(0).start()
 
     @pl.loop(1, ny)
     def _(k):
@@ -334,6 +399,8 @@
         term_z(k).start()
 
     back_hubs_ref[at(z, hub), :] = back_sum_ref[at(z, hub), :]
+
+    pair_sum(0)
 
     for i in range(height // lanes):
         count_ref[:, lanes * i : lanes * (i + 1)] = jnp.transpose(
@@ -367,29 +434,27 @@
         near += [k, nz - k]
     near.append(nz // 2)
     plane = ny * cap
-    for dz in near:
-
-        @pl.loop(max(dz * ny, 1), (dz + 1) * ny)
-        def _(k):
-            forth_in(k).wait_recv()
-
-        src = z_at(-dz)
-
-        @pl.loop(0, rows // step)
-        def _(i):
-            span = at(i, step)
-            c = count_ref[span, pl.ds(pl.multiple_of(rows + nhub + src * plane, plane), plane)]
-            total = total_ref[span, :] + dot(c, recv_ref[at(src, plane), :])
-            if dz != near[-1]:
-                total_ref[span, :] = total
-            else:
-                agg_ref[span, :] = (total * by_vertex(span)).astype(BF16)
+    def planes(pair_of, arrived, lhs_ref, start, rhs_ref):
+        for dz in pair_of:
+
+            @pl.loop(max(dz * ny, 1), (dz + 1) * ny)
+            def _(k):
+                arrived(k).wait_recv()
+
+        at_z = [z_at(-dz) for dz in pair_of]
+        c = [lhs_ref[:, pl.ds(pl.multiple_of(start + q * plane, plane), plane)] for q in at_z]
+        r = [rhs_ref[at(q, plane), :] for q in at_z]
+        return dot(jnp.concatenate(c, axis=1), jnp.concatenate(r, axis=0))
+
+    turns = [near[i : i + 2] for i in range(0, nz, 2)]
+    for turn in turns[:-1]:
+        total_ref[...] += planes(turn, forth_in, count_ref, rows + nhub, recv_ref)
+    total = total_ref[...] + planes(turns[-1], forth_in, count_ref, rows + nhub, recv_ref)
+    agg_ref[...] = (total * by_vertex(slice(None))).astype(BF16)
 
     put_dw(1, agg_ref)
-
-    @pl.loop(1, groups)
-    def _(k):
-        dw_copy(k, 1).start()
+    pair(1).start()
+    pair_sum(1)
 
     @pl.loop(0, rows // step)
     def _(i):
@@ -398,16 +463,14 @@
 
     for m in range(2):
 
-        @pl.loop(1, groups)
+        @pl.loop(1, nx)
         def _(k):
             dw_in(k, m).wait_recv()
-
-        dw_recv_ref[m, lane] = dw_ref[m, lane]
 
         @pl.loop(0, parts)
         def _(q):
             total = dw_recv_ref[m, 0, q]
-            for p in range(1, groups):
+            for p in range(1, nx):
                 total = total + dw_recv_ref[m, p, q]
             slab_ref[lax.rem(q, ny), q // ny, m] = total
 
@@ -481,25 +544,11 @@
         spot = fin_recv_ref.at[d_at(-k)]
         return remote(spot, spot, e_send.at[k], e_recv.at[k], {"dp": d_at(k)})
 
-    for dz in near:
-
-        @pl.loop(max(dz * ny, 1), (dz + 1) * ny)
-        def _(k):
-            back_in(k).wait_recv()
-
-        if dz == near[-1]:
-            finish_weights()
-        src = z_at(-dz)
-
-        @pl.loop(0, rows // step)
-        def _(i):
-            span = at(i, step)
-            c = spread_ref[span, at(src, plane)]
-            total = grad_ref[span, :] + dot(c, back_recv_ref[at(src, plane), :])
-            if dz != near[-1]:
-                grad_ref[span, :] = total
-            else:
-                gf_ref[span, :] = total.astype(BF16)
+    for turn in turns[:-1]:
+        grad_ref[...] += planes(turn, back_in, spread_ref, 0, back_recv_ref)
+    finish_weights()
+    total = grad_ref[...] + planes(turns[-1], back_in, spread_ref, 0, back_recv_ref)
+    gf_ref[...] = total.astype(BF16)
 
     @pl.loop(1, groups)
     def _(k):
@@ -528,11 +577,21 @@
         term_y(k).wait_send()
         slab_y(k).wait_send()
 
+    for m in range(2):
+        pair(m).wait_send()
+
+        @pl.loop(1, nx)
+        def _(k):
+            dw_copy(k, m).wait_send()
+
     @pl.loop(1, groups)
     def _(k):
-        dw_copy(k, 0).wait_send()
-        dw_copy(k, 1).wait_send()
         fin(k).wait_send()
+
+
+def publish(*refs):
+    for src, dst in zip(refs[:4], refs[4:]):
+        dst[...] = src[...]
 
 
 def shards(feats, grad_out, w_self, w_neigh, nbr, deg, hub_rows, send_rows):
@@ -548,6 +607,7 @@
     height = rows + nhub + sent
     ny = COLUMNS
     nz = parts // ny
+    nx = groups // 2
     scale = float((groups * parts * rows) ** -0.5)
     vmem = pltpu.VMEM
     dma = pltpu.SemaphoreType.DMA
@@ -559,9 +619,17 @@
             jax.ShapeDtypeStruct((width // parts, width), F32),
             jax.ShapeDtypeStruct((width // parts, width), F32),
         ),
-        in_specs=[pl.BlockSpec(memory_space=vmem)] * 8,
+        in_specs=[pl.BlockSpec(memory_space=pl.ANY)] * 8,
         out_specs=[pl.BlockSpec(memory_space=vmem)] * 4,
         scratch_shapes=[
+            vmem((rows, width), BF16),
+            vmem((rows, width), BF16),
+            vmem((width, width), BF16),
+            vmem((width, width), BF16),
+            vmem((slots, 1, rows), jnp.int32),
+            vmem((1, rows), jnp.int32),
+            vmem((parts, cap), jnp.int32),
+            vmem((1, hub), jnp.int32),
             vmem((sent // 128 + 1, 128), jnp.int32),
             vmem((slots, rows), jnp.int32),
             vmem((sent + hub, rows), BF16),
@@ -585,8 +653,9 @@
             vmem((rows, width), F32),
             vmem((rows, width), BF16),
             vmem((rows, 128), F32),
-            vmem((2, groups, parts, 8, 128), F32),
-            vmem((2, groups, parts, 8, 128), F32),
+            vmem((2, 2, nx, parts, 8, 128), F32),
+            vmem((2, nx, parts, 8, 128), F32),
+            vmem((2, nx, parts, 8, 128), F32),
             vmem((ny, nz, 2, 8, 128), F32),
             vmem((ny, nz, 2, 8, 128), F32),
             vmem((nz, 2, 8, 128), F32),
@@ -594,10 +663,11 @@
             vmem((2, 8, 128), F32),
             vmem((groups, 2, 8, 128), F32),
         ]
+        + [dma((8,))]
         + [dma((parts,))] * 4
         + ([dma((nz,))] * 2 + [dma((ny,))] * 2)
         + ([dma((ny,))] * 2 + [dma((nz,))] * 2)
-        + [dma((2, groups))] * 2
+        + ([dma((2,))] * 2 + [dma((2, nx))] * 2)
         + ([dma((ny,))] * 2 + [dma((nz,))] * 2)
         + [dma((groups,))] * 2,
         compiler_params=pltpu.CompilerParams(collective_id=0, has_side_effects=True),
@@ -611,7 +681,12 @@
         send_rows[0, 0],
         hub_rows,
     )
-    out, grad_feats, grad_w_self, grad_w_neigh = outs
+    out, grad_feats, grad_w_self, grad_w_neigh = pl.pallas_call(
+        publish,
+        out_shape=tuple(jax.ShapeDtypeStruct(a.shape, a.dtype) for a in outs),
+        in_specs=[pl.BlockSpec(memory_space=vmem)] * 4,
+        out_specs=[pl.BlockSpec(memory_space=vmem)] * 4,
+    )(*outs)
     return (out[None], grad_feats[None], grad_w_self, grad_w_neigh)
 
 

time: 85.7 us -> 79.3 us (0.925)
  local copies, waits for them, and re-layouts: 4.11 us -> 0 us
  Pallas kernels: 80.8 us -> 78.5 us
    pallas_call x1, Pallas kernels: 80.8 us -> 76.3 us  [shards(): pl.pallas_call(functools.partial(layer_kernel, parts, groups, scale), out...]
    unnamed x10 -> x0, local copies, waits for them, and re-layouts: 4.11 us -> none
    pallas_call x0 -> x1, Pallas kernels: none -> 2.21 us  [shards(): pl.pallas_call(publish, out_shape=tuple((jax.ShapeDtypeStruct(a.shape, a....]
where the time goes in v3:
time: 79.3 us; the launch traced here: 79.2 us
  Pallas kernels  78.5 us (99%)
    pallas_call x1, Pallas kernels, shards(): pl.pallas_call(functools.partial(layer_kernel, parts, groups, scale), out...  76.3 us
    pallas_call x1, Pallas kernels, shards(): pl.pallas_call(publish, out_shape=tuple((jax.ShapeDtypeStruct(a.shape, a....  2.21 us

profile of v3, /device:TPU:1, one launch (start us, length us, event | category | flops | bytes accessed | tf_op | source)
XLA Modules:
  0.0 79.2 jit_solution(5024612434920006960)
XLA Ops:
  0.6 76.3 %shard_map.111 = (bf16[512,512]{1,0:T(8,128)(2,1)}, bf16[512,512]{1,0:T(8,128)(2,1)}, f32[16,512]{1,0:T(8,128)}, f32[16,512]{1,0:T(8,128)}) custom-call(bf16[512,512]{1,0:T(8,128)(2,1)} %bitcast.6, bf16[512,512]{1,0:T(8,128)(2,1)} %bitcast.7, bf16[512,512]{1,0:T(8,128)(2,1)} %ws_hbm.1, bf16[512,512]{1,0:T(8,128)(2,1)} %wn_hbm.1, s32[10,1,512]{2,1,0:T(1,128)} %bitcast.8, ...), custom_call_target="tpu_custom_call" | custom-call | tf_op jit(solution)/shard_map/pallas_call | solution.py:614
  77.0 2.2 %shard_map.112 = (bf16[512,512]{1,0:T(8,128)(2,1)}, bf16[512,512]{1,0:T(8,128)(2,1)}, f32[16,512]{1,0:T(8,128)}, f32[16,512]{1,0:T(8,128)}) custom-call(bf16[512,512]{1,0:T(8,128)(2,1)} %get-tuple-element.12.refs_0_, bf16[512,512]{1,0:T(8,128)(2,1)} %get-tuple-element.13.refs_1_, f32[16,512]{1,0:T(8,128)} %get-tuple-element.14.refs_2_, ...), custom_call_target="tpu_custom_call" | custom-call | tf_op jit(solution)/shard_map/pallas_call | solution.py:684
